TPU v7x, 128 devices: a whole 4x4x4 slice. The times are simulated.
128 devices in a mesh: expert: 64 (over x, y, z), dp: 2 (over core).
Axes of the slice: x: 4, y: 4, z: 4, core: 2. Of those that a mesh axis runs over, the one named last changes fastest.
Arguments:
- tokens: bfloat16 [12288, 4096], P(('expert', 'dp')), may hold values from -6 to 6
- w_gate: bfloat16 [128, 4096, 768], P(('expert', 'dp')), may hold values from -0.09375 to 0.09375
- w_up: bfloat16 [128, 4096, 768], P(('expert', 'dp')), may hold values from -0.09375 to 0.09375
- w_down: bfloat16 [128, 768, 4096], P(('expert', 'dp')), may hold values from -0.21875 to 0.21875
- route_ids: int32 [12288, 8], P(('expert', 'dp')), may hold values from 0 to 127, all different within a row
- route_gates: float32 [12288, 8], P(('expert', 'dp')), may hold values from 0.05 to 0.4
- hot_experts: int32 [1], replicated, may hold values from 0 to 127
Outputs:
- mixed: bfloat16 [12288, 4096], P(('expert', 'dp'))
Inputs may be any that keep to these rules, and one draw needn't show every extreme that they name: `route_ids`: each row names 8 different experts.
All inputs are finite; a program needn't handle non-finite values.
Results may differ from a plain program's by a relative error of at most 0.007.
Values may be sent and summed in bfloat16 or wider, within the bound.
A program may use at most 192 MiB of HBM per device.

v0:
```python
import jax
import jax.numpy as jnp
from jax import lax
from jax.sharding import PartitionSpec as P

CAP = 6


def expert_ffn(in_rows, gate_w, up_w, down_w):
    gate_val = jnp.dot(in_rows, gate_w, preferred_element_type=jnp.float32)
    up_val = jnp.dot(in_rows, up_w, preferred_element_type=jnp.float32)
    hidden = (jax.nn.silu(gate_val) * up_val).astype(jnp.bfloat16)
    return jnp.dot(hidden, down_w, preferred_element_type=jnp.float32).astype(jnp.bfloat16)


def on_device(tokens, w_gate, w_up, w_down, route_ids, route_gates, hot_experts):
    feat_width = tokens.shape[1]
    tok_rows = tokens.shape[0]
    top_k = route_ids.shape[1]
    n_dp = lax.axis_size("dp")
    experts = lax.axis_size("expert") * n_dp
    hot_id = hot_experts[0]
    me = lax.axis_index("expert") * n_dp + lax.axis_index("dp")
    own = (w_gate[0], w_up[0], w_down[0])
    with jax.named_scope("hot_weight_broadcast"):
        is_root = me == hot_id
        hot_w = tuple(
            (lax.psum(jnp.where(is_root, w, jnp.zeros_like(w)), ("expert", "dp")) for w in own)
        )
    with jax.named_scope("routing"):
        flat_ids = route_ids.reshape(-1)
        labels = lax.iota(jnp.int32, experts)
        onehot = (flat_ids[:, None] == labels[None, :]).astype(jnp.int32)
        rank_of = jnp.sum(onehot * (jnp.cumsum(onehot, axis=0) - 1), axis=1)
        is_kept = (flat_ids != hot_id) & (rank_of < CAP)
        slot_of = jnp.where(is_kept, flat_ids * CAP + rank_of, experts * CAP)
        slots = lax.iota(jnp.int32, experts * CAP)
        hit = slot_of[None, :] == slots[:, None]
        dispatch = jnp.any(hit.reshape(experts * CAP, tok_rows, top_k), axis=2)
    with jax.named_scope("dispatch"):
        outgoing = jnp.dot(
            dispatch.astype(tokens.dtype), tokens, preferred_element_type=jnp.float32
        ).astype(tokens.dtype)
        to_send = outgoing.reshape(experts, CAP * feat_width)
        arrived = lax.all_to_all(to_send, ("expert", "dp"), 0, 0, tiled=True)
    with jax.named_scope("expert_ffn"):
        results = expert_ffn(arrived.reshape(-1, feat_width), *own)
    with jax.named_scope("return"):
        come_back = lax.all_to_all(
            results.reshape(experts, CAP * feat_width), ("expert", "dp"), 0, 0, tiled=True
        )
        returned = come_back.reshape(experts * CAP, feat_width)
    with jax.named_scope("combine"):
        gate_flat = route_gates.reshape(-1)
        cold_weight = jnp.where(is_kept, gate_flat, jnp.zeros_like(gate_flat))
        weight_of_slot = jnp.where(hit, cold_weight[None, :], 0.0)
        combine = jnp.sum(weight_of_slot.reshape(experts * CAP, tok_rows, top_k), axis=2).T
        cold_sum = jnp.dot(
            combine,
            returned.astype(jnp.float32),
            precision=lax.Precision.HIGHEST,
            preferred_element_type=jnp.float32,
        )
    with jax.named_scope("hot_expert"):
        hot_out = expert_ffn(tokens, *hot_w)
        hot_weight = jnp.sum(
            jnp.where(route_ids == hot_id, route_gates, jnp.zeros_like(route_gates)), axis=1
        )
        combined = cold_sum + hot_weight[:, None] * hot_out.astype(jnp.float32)
    return combined.astype(jnp.bfloat16)


def solution(mesh):
    in_specs = (
        P(("expert", "dp"), None),
        P(("expert", "dp"), None, None),
        P(("expert", "dp"), None, None),
        P(("expert", "dp"), None, None),
        P(("expert", "dp"), None),
        P(("expert", "dp"), None),
        P(),
    )
    out_specs = P(("expert", "dp"), None)
    return jax.shard_map(
        on_device, mesh=mesh, in_specs=in_specs, out_specs=out_specs, check_vma=False
    )
```

profile of v0, /device:TPU:0, one launch (start us, length us, event | category | flops | bytes accessed | tf_op | source)
XLA Modules:
  0.0 559.9 jit_solution(3620452224844530923)
XLA Ops:
  6.5 0.9 copy.64
  8.3 0.2 fusion.13
  8.7 0.3 fusion.15
  9.2 0.7 add_select_fusion
  10.0 0.8 fusion.8
  10.8 4.5 convolution_convert_fusion
  15.2 23.8 %all_to_all.16 = bf16[128,1,24576]{2,1,0:T(2,128)(2,1)} reshape(bf16[768,4096]{1,0:T(8,128)(2,1)} %convolution_convert_fusion) | data formatting | bytes 12582912 | tf_op jit(solution)/shard_map/dispatch/all_to_all | solution.py:45
  39.0 0.5 broadcast.85
  39.4 38.9 %reduce.2 = bf16[128,24576]{1,0:T(8,128)(2,1)} reduce(bf16[128,1,24576]{2,1,0:T(2,128)(2,1)} %all_to_all.16, bf16[]{:T(256)} %broadcast.85), dimensions={1}, to_apply=%all_to_all.16.reduce_sub_computation | reduce | bytes 12582914 | tf_op jit(solution)/shard_map/dispatch/all_to_all | solution.py:45
  78.3 9.4 %reshape.90 = bf16[128,2,12288]{2,1,0:T(2,128)(2,1)} reshape(bf16[128,24576]{1,0:T(8,128)(2,1)} %reduce.2) | data formatting | bytes 12582912
  87.7 11.6 %all-to-all-start = ((bf16[128,2,12288]{2,1,0:T(2,128)(2,1)}), bf16[128,2,12288]{2,1,0:T(2,128)(2,1)}, u32[]{:S(2)}, u32[]{:S(2)}) async-start(bf16[128,2,12288]{2,1,0:T(2,128)(2,1)} %reshape.90), calls=%async_computation | async-start | bytes 12582912 | tf_op jit(solution)/shard_map/dispatch/all_to_all | solution.py:45
  99.4 5.9 %bitcast_select_fusion = bf16[768,4096]{1,0:T(8,128)(2,1)} fusion(bf16[1,768,4096]{2,1,0:T(8,128)(2,1)} %param.10, pred[]{:T(512)S(6)} %eq.59), kind=kLoop, calls=%fused_computation.2 | loop fusion | flops 3145728 | bytes 12582913 | tf_op jit(solution)/shard_map/hot_weight_broadcast/jit(_where)/select_n | solution.py:28
  105.3 9.9 %bitcast_select_fusion.1 = (bf16[4096,768]{1,0:T(8,128)(2,1)}, bf16[4096,768]{1,0:T(8,128)(2,1)}) fusion(bf16[1,4096,768]{2,1,0:T(8,128)(2,1)} %param.9, pred[]{:T(512)S(6)} %eq.59, bf16[1,4096,768]{2,1,0:T(8,128)(2,1)} %param.8), kind=kLoop, calls=%fused_computation.4 | loop fusion | flops 6291456 | bytes 25165824 | tf_op jit(solution)/shard_map/hot_weight_broadcast/jit(_where)/select_n | solution.py:28
  115.1 65.2 %all-to-all-done = bf16[128,2,12288]{2,1,0:T(2,128)(2,1)} async-done(((bf16[128,2,12288]{2,1,0:T(2,128)(2,1)}), bf16[128,2,12288]{2,1,0:T(2,128)(2,1)}, u32[]{:S(2)}, u32[]{:S(2)}) %all-to-all-start) | async-done | bytes 6291488 | tf_op jit(solution)/shard_map/dispatch/all_to_all | solution.py:45
  180.4 34.5 %reshape.91 = bf16[128,1,24576]{2,1,0:T(2,128)(2,1)} reshape(bf16[128,2,12288]{2,1,0:T(2,128)(2,1)} %all-to-all-done) | data formatting | bytes 12582912
  214.8 38.3 %reduce = bf16[128,24576]{1,0:T(8,128)(2,1)} reduce(bf16[128,1,24576]{2,1,0:T(2,128)(2,1)} %reshape.91, bf16[]{:T(256)} %constant.43), dimensions={1}, to_apply=%all_to_all.13.reduce_sub_computation | reduce | bytes 12582914 | tf_op jit(solution)/shard_map/dispatch/all_to_all | solution.py:45
  253.2 11.2 %reshape.86 = bf16[768,4096]{1,0:T(8,128)(2,1)} reshape(bf16[128,24576]{1,0:T(8,128)(2,1)} %reduce) | data formatting | bytes 12582912 | tf_op jit(solution)/shard_map/expert_ffn/reshape | solution.py:47
  264.4 9.1 %fusion.3 = f32[768,768]{1,0:T(8,128)S(1)} fusion(bf16[768,4096]{1,0:T(8,128)(2,1)} %reshape.86, bf16[1,4096,768]{2,1,0:T(8,128)(2,1)} %param.8), kind=kOutput, calls=%fused_computation.8 | convolution fusion | flops 4831838208 | bytes 14942208 | tf_op jit(solution)/shard_map/expert_ffn/dot_general | solution.py:10
  273.5 8.0 %multiply_convert_fusion = bf16[768,768]{1,0:T(8,128)(2,1)S(1)} fusion(f32[768,768]{1,0:T(8,128)S(1)} %fusion.3, bf16[768,4096]{1,0:T(8,128)(2,1)S(1)} %copy-done.1, bf16[1,4096,768]{2,1,0:T(8,128)(2,1)} %param.9), kind=kOutput, calls=%fused_computation.15 | convolution fusion | flops 4835377152 | bytes 16121856 | tf_op jit(solution)/shard_map/expert_ffn/dot_general | solution.py:11
  281.6 7.1 %convolution_convert_fusion.1 = bf16[768,4096]{1,0:T(8,128)(2,1)} fusion(bf16[768,768]{1,0:T(8,128)(2,1)S(1)} %multiply_convert_fusion, bf16[1,768,4096]{2,1,0:T(8,128)(2,1)S(1)} %bitcast.50), kind=kOutput, calls=%fused_computation.1 | convolution fusion | flops 4834983936 | bytes 13762560 | tf_op jit(solution)/shard_map/expert_ffn/dot_general | solution.py:13
  288.7 23.9 %all_to_all.17 = bf16[128,1,24576]{2,1,0:T(2,128)(2,1)} reshape(bf16[768,4096]{1,0:T(8,128)(2,1)} %convolution_convert_fusion.1) | data formatting | bytes 12582912 | tf_op jit(solution)/shard_map/return/all_to_all | solution.py:49
  312.5 38.8 %reduce.3 = bf16[128,24576]{1,0:T(8,128)(2,1)} reduce(bf16[128,1,24576]{2,1,0:T(2,128)(2,1)} %all_to_all.17, bf16[]{:T(256)} %broadcast.85), dimensions={1}, to_apply=%all_to_all.17.reduce_sub_computation | reduce | bytes 12582914 | tf_op jit(solution)/shard_map/return/all_to_all | solution.py:49
  351.4 9.7 %reshape.92 = bf16[128,2,12288]{2,1,0:T(2,128)(2,1)} reshape(bf16[128,24576]{1,0:T(8,128)(2,1)} %reduce.3) | data formatting | bytes 12582912
  361.1 7.8 %all-to-all-start.1 = ((bf16[128,2,12288]{2,1,0:T(2,128)(2,1)}), bf16[128,2,12288]{2,1,0:T(2,128)(2,1)}, u32[]{:S(2)}, u32[]{:S(2)}) async-start(bf16[128,2,12288]{2,1,0:T(2,128)(2,1)} %reshape.92), calls=%async_computation.1 | async-start | bytes 12582912 | tf_op jit(solution)/shard_map/return/all_to_all | solution.py:49
  369.0 0.8 select_reduce_fusion
  369.8 81.9 %all-reduce.3.cloned.1.call-done = (bf16[768,4096]{1,0:T(8,128)(2,1)}, bf16[4096,768]{1,0:T(8,128)(2,1)}, bf16[4096,768]{1,0:T(8,128)(2,1)}) async-done(((bf16[768,4096]{1,0:T(8,128)(2,1)}, bf16[4096,768]{1,0:T(8,128)(2,1)}, bf16[4096,768]{1,0:T(8,128)(2,1)}), (bf16[768,4096]{1,0:T(8,128)(2,1)}, bf16[4096,768]{1,0:T(8,128)(2,1)}, bf16[4096,768]{1,0:T(8,128)(2,1)})) %all-reduce.3.cloned.1.call-update) | async-done | bytes 18874384 | tf_op jit(solution)/shard_map/hot_weight_broadcast/psum | solution.py:28
  451.7 3.9 convolution_bitcast_fusion.1
  455.6 7.1 %fusion.7 = f32[96,4096]{1,0:T(8,128)S(1)} fusion(bf16[768,4096]{1,0:T(8,128)(2,1)} %get-tuple-element.5, bf16[96,4096]{1,0:T(8,128)(2,1)S(1)} %copy-done, bf16[4096,768]{1,0:T(8,128)(2,1)} %get-tuple-element.6, f32[96]{0:T(128)S(1)} %get-tuple-element.9, f32[96,768]{1,0:T(8,128)S(1)} %convolution_bitcast_fusion.1), kind=kOutput, calls=%fused_computation.14 | convolution fusion | flops 1209581568 | bytes 15237504 | tf_op jit(solution)/shard_map/hot_expert/dot_general | solution.py:13
  462.8 33.8 %reshape.93 = bf16[128,1,24576]{2,1,0:T(2,128)(2,1)} reshape(bf16[128,2,12288]{2,1,0:T(2,128)(2,1)} %all-to-all-done.1) | data formatting | bytes 12582912
  496.6 38.3 %reduce.1 = bf16[128,24576]{1,0:T(8,128)(2,1)} reduce(bf16[128,1,24576]{2,1,0:T(2,128)(2,1)} %reshape.93, bf16[]{:T(256)} %constant.43), dimensions={1}, to_apply=%all_to_all.15.reduce_sub_computation | reduce | bytes 12582914 | tf_op jit(solution)/shard_map/return/all_to_all | solution.py:49
  534.9 11.1 %reshape.87 = bf16[768,4096]{1,0:T(8,128)(2,1)} reshape(bf16[128,24576]{1,0:T(8,128)(2,1)} %reduce.1) | data formatting | bytes 12582912 | tf_op jit(solution)/shard_map/return/reshape | solution.py:52
  546.0 6.8 %fusion.5 = bf16[96,4096]{1,0:T(8,128)(2,1)} fusion(f32[96,4096]{1,0:T(8,128)S(1)} %fusion.7, f32[768,96]{0,1:T(8,128)S(1)} %select_reduce_fusion, bf16[768,4096]{1,0:T(8,128)(2,1)} %reshape.87), kind=kOutput, calls=%fused_computation.11 | convolution fusion | flops 3624665088 | bytes 8945664 | tf_op jit(solution)/shard_map/combine/dot_general | solution.py:58
  (28 shorter events, 0.9 us)
Async XLA Ops:
  6.5 4.2 copy-start
  87.7 92.7 %all-to-all-start = ((bf16[128,2,12288]{2,1,0:T(2,128)(2,1)}), bf16[128,2,12288]{2,1,0:T(2,128)(2,1)}, u32[]{:S(2)}, u32[]{:S(2)}) async-start(bf16[128,2,12288]{2,1,0:T(2,128)(2,1)} %reshape.90), calls=%async_computation | async-start | bytes 12582912 | tf_op jit(solution)/shard_map/dispatch/all_to_all | solution.py:45
  99.3 352.4 %all-reduce.3.cloned.1.call-start = ((), (), s32[]{:S(2)}) async-start(), calls=%async_computation.2 | async-start | bytes 37748736 | tf_op jit(solution)/shard_map/hot_weight_broadcast/psum | solution.py:28
  253.2 28.4 %slice-start = ((s8[6291456]{0:T(1024)(128)(4,1)}), s8[2097152]{0:T(1024)(128)(4,1)S(1)}, s32[]{:S(2)}) async-start(s8[6291456]{0:T(1024)(128)(4,1)} %bitcast.49), calls=%async_computation.3 | async-start | bytes 4194304
  264.4 9.1 %copy-start.1 = (bf16[768,4096]{1,0:T(8,128)(2,1)S(1)}, bf16[768,4096]{1,0:T(8,128)(2,1)}, u32[]{:S(2)}) copy-start(bf16[768,4096]{1,0:T(8,128)(2,1)} %reshape.86) | copy-start | bytes 18874372
  264.4 17.2 %slice-start.1 = ((s8[6291456]{0:T(1024)(128)(4,1)}), s8[4194304]{0:T(1024)(128)(4,1)S(1)}, s32[]{:S(2)}) async-start(s8[6291456]{0:T(1024)(128)(4,1)} %bitcast.49), calls=%async_computation.4 | async-start | bytes 8388608
  361.1 7.8 %copy-start.2 = (s32[96,8]{0,1:T(8,128)S(1)}, s32[96,8]{0,1:T(8,128)}, u32[]{:S(2)}) copy-start(s32[96,8]{0,1:T(8,128)} %param.11) | copy-start | bytes 9220
  361.1 7.8 %copy-start.3 = (f32[96,8]{0,1:T(8,128)S(1)}, f32[96,8]{0,1:T(8,128)}, u32[]{:S(2)}) copy-start(f32[96,8]{0,1:T(8,128)} %param.12) | copy-start | bytes 9220
  361.1 101.7 %all-to-all-start.1 = ((bf16[128,2,12288]{2,1,0:T(2,128)(2,1)}), bf16[128,2,12288]{2,1,0:T(2,128)(2,1)}, u32[]{:S(2)}, u32[]{:S(2)}) async-start(bf16[128,2,12288]{2,1,0:T(2,128)(2,1)} %reshape.92), calls=%async_computation.1 | async-start | bytes 12582912 | tf_op jit(solution)/shard_map/return/all_to_all | solution.py:49
Sparse Core Ops, SparseCore 0:
  115.3 336.3 all-reduce.2
where the time goes:
time: 571 us; the launch traced here: 560 us
  other arithmetic  173 us (30%)
  local copies, waits for them, and re-layouts  159 us (28%)
  waiting for transfers between devices  147 us (26%)
  matrix products  46.5 us (8%)
  starting transfers between devices  19.5 us (3%)
  between operations  14.5 us (3%)
    unnamed x17, local copies, waits for them, and re-layouts  88.2 us
    psum x1, waiting for transfers between devices, on_device(): lax.psum(jnp.where(is_root, w, jnp.zeros_like(w)), ('expert', 'dp'))  81.9 us
    all_to_all x2, other arithmetic, on_device(): arrived = lax.all_to_all(to_send, ('expert', 'dp'), 0, 0, tiled=True)  77.2 us
    all_to_all x2, other arithmetic, on_device(): lax.all_to_all(results.reshape(experts, CAP * feat_width), ('expert', 'dp...  77.2 us
    all_to_all x1, waiting for transfers between devices, on_device(): arrived = lax.all_to_all(to_send, ('expert', 'dp'), 0, 0, tiled=True)  65.2 us
    all_to_all x2, local copies, waits for them, and re-layouts, on_device(): arrived = lax.all_to_all(to_send, ('expert', 'dp'), 0, 0, tiled=True)  24.2 us
    all_to_all x1, local copies, waits for them, and re-layouts, on_device(): lax.all_to_all(results.reshape(experts, CAP * feat_width), ('expert', 'dp...  23.9 us
    select_n x2, other arithmetic, on_device(): jnp.where(is_root, w, jnp.zeros_like(w))  15.8 us
  transfers between devices with their start and end apart: 3, of which 2 were waited for; matrix products, arithmetic and copies ran while one was open for 33% of the time, Pallas kernels for 0%

commit v1 on v0

--- a/solution.py
+++ b/solution.py
@@ -24,8 +24,14 @@
     own = (w_gate[0], w_up[0], w_down[0])
     with jax.named_scope("hot_weight_broadcast"):
         is_root = me == hot_id
+        deliver_the_turns = lambda buf, lane_axis, chip_axis: lax.psum(
+            lax.psum(buf, lane_axis), chip_axis
+        )
         hot_w = tuple(
-            (lax.psum(jnp.where(is_root, w, jnp.zeros_like(w)), ("expert", "dp")) for w in own)
+            (
+                deliver_the_turns(jnp.where(is_root, w, jnp.zeros_like(w)), "expert", "dp")
+                for w in own
+            )
         )
     with jax.named_scope("routing"):
         flat_ids = route_ids.reshape(-1)

time: 571 us -> 798 us (1.40)
  waiting for transfers between devices: 147 us -> 304 us
  blocking collectives: 0 us -> 83.3 us
  starting transfers between devices: 19.5 us -> 6.95 us
    psum x1 -> x2, waiting for transfers between devices: 81.9 us -> 229 us  [the longest x1 229 us: on_device(): lax.psum(buf, lane_axis)]
    all_to_all x0 -> x1, blocking collectives: none -> 83.3 us  [on_device(): arrived = lax.all_to_all(to_send, ('expert', 'dp'), 0, 0, tiled=True)]
    all_to_all x1, waiting for transfers between devices: 0.01 us -> 74.8 us  [on_device(): lax.all_to_all(results.reshape(experts, CAP * feat_width), ('expert', 'dp...]
    all_to_all x1 -> x0, waiting for transfers between devices: 65.2 us -> none  [on_device(): arrived = lax.all_to_all(to_send, ('expert', 'dp'), 0, 0, tiled=True)]
    all_to_all x1 -> x0, starting transfers between devices: 11.6 us -> none  [on_device(): arrived = lax.all_to_all(to_send, ('expert', 'dp'), 0, 0, tiled=True)]
  transfers between devices with their start and end apart: 3 -> 3, of which waited for: 2 -> 2; matrix products, arithmetic and copies ran while one was open for 33% -> 38% of each run, Pallas kernels for 0% -> 0%
where the time goes in v1:
time: 798 us; the launch traced here: 786 us
  waiting for transfers between devices  304 us (38%)
  other arithmetic  172 us (22%)
  local copies, waits for them, and re-layouts  159 us (20%)
  blocking collectives  83.3 us (10%)
  matrix products  46.5 us (6%)
  between operations  14.5 us (2%)
    psum x1, waiting for transfers between devices, on_device(): lax.psum(buf, lane_axis)  229 us
    unnamed x17, local copies, waits for them, and re-layouts  87.1 us
    all_to_all x1, blocking collectives, on_device(): arrived = lax.all_to_all(to_send, ('expert', 'dp'), 0, 0, tiled=True)  83.3 us
    all_to_all x2, other arithmetic, on_device(): arrived = lax.all_to_all(to_send, ('expert', 'dp'), 0, 0, tiled=True)  77.1 us
    all_to_all x2, other arithmetic, on_device(): lax.all_to_all(results.reshape(experts, CAP * feat_width), ('expert', 'dp...  77.1 us
    all_to_all x1, waiting for transfers between devices, on_device(): lax.all_to_all(results.reshape(experts, CAP * feat_width), ('expert', 'dp...  74.8 us
    all_to_all x2, local copies, waits for them, and re-layouts, on_device(): arrived = lax.all_to_all(to_send, ('expert', 'dp'), 0, 0, tiled=True)  25.2 us
    all_to_all x1, local copies, waits for them, and re-layouts, on_device(): lax.all_to_all(results.reshape(experts, CAP * feat_width), ('expert', 'dp...  23.8 us
  transfers between devices with their start and end apart: 3, of which 2 were waited for; matrix products, arithmetic and copies ran while one was open for 38% of the time, Pallas kernels for 0%

profile of v1, /device:TPU:0, one launch (start us, length us, event | category | flops | bytes accessed | tf_op | source)
XLA Modules:
  0.0 786.3 jit_solution(15046526941626902069)
XLA Ops:
  7.3 5.9 bitcast_select_fusion
  13.1 10.0 %bitcast_select_fusion.1 = (bf16[4096,768]{1,0:T(8,128)(2,1)}, bf16[4096,768]{1,0:T(8,128)(2,1)}) fusion(bf16[1,4096,768]{2,1,0:T(8,128)(2,1)} %param.9, pred[]{:T(512)S(6)} %eq.59, bf16[1,4096,768]{2,1,0:T(8,128)(2,1)} %param.8), kind=kLoop, calls=%fused_computation.4 | loop fusion | flops 6291456 | bytes 25165824 | tf_op jit(solution)/shard_map/hot_weight_broadcast/jit(_where)/select_n | solution.py:32
  23.2 0.6 copy-done.2
  24.0 0.1 copy.66
  24.1 0.2 fusion.13
  24.4 228.8 %all-reduce.5.cloned.1.call-done = (bf16[768,4096]{1,0:T(8,128)(2,1)}, bf16[4096,768]{1,0:T(8,128)(2,1)}, bf16[4096,768]{1,0:T(8,128)(2,1)}) async-done(((bf16[768,4096]{1,0:T(8,128)(2,1)}, bf16[4096,768]{1,0:T(8,128)(2,1)}, bf16[4096,768]{1,0:T(8,128)(2,1)}), (bf16[768,4096]{1,0:T(8,128)(2,1)}, bf16[4096,768]{1,0:T(8,128)(2,1)}, bf16[4096,768]{1,0:T(8,128)(2,1)})) %all-reduce.5.cloned.1.call-update) | async-done | bytes 18874384 | tf_op jit(solution)/shard_map/hot_weight_broadcast/psum | solution.py:28
  253.5 0.3 fusion.15
  254.0 0.8 fusion.8
  254.8 4.4 convolution_convert_fusion
  259.2 24.7 %all_to_all.16 = bf16[128,1,24576]{2,1,0:T(2,128)(2,1)} reshape(bf16[768,4096]{1,0:T(8,128)(2,1)} %convolution_convert_fusion) | data formatting | bytes 12582912 | tf_op jit(solution)/shard_map/dispatch/all_to_all | solution.py:51
  284.0 0.5 broadcast.85
  284.5 38.9 %reduce.2 = bf16[128,24576]{1,0:T(8,128)(2,1)} reduce(bf16[128,1,24576]{2,1,0:T(2,128)(2,1)} %all_to_all.16, bf16[]{:T(256)} %broadcast.85), dimensions={1}, to_apply=%all_to_all.16.reduce_sub_computation | reduce | bytes 12582914 | tf_op jit(solution)/shard_map/dispatch/all_to_all | solution.py:51
  323.3 9.4 %reshape.90 = bf16[128,2,12288]{2,1,0:T(2,128)(2,1)} reshape(bf16[128,24576]{1,0:T(8,128)(2,1)} %reduce.2) | data formatting | bytes 12582912
  332.7 83.3 %all_to_all.20 = bf16[128,2,12288]{2,1,0:T(2,128)(2,1)} all-to-all(bf16[128,2,12288]{2,1,0:T(2,128)(2,1)} %reshape.90), channel_id=1, replica_groups=mesh['expert'=64,'dp'=2] {'expert','dp'}, dimensions={0} | all-to-all | bytes 12582912 | tf_op jit(solution)/shard_map/dispatch/all_to_all | solution.py:51
  416.0 33.8 %reshape.91 = bf16[128,1,24576]{2,1,0:T(2,128)(2,1)} reshape(bf16[128,2,12288]{2,1,0:T(2,128)(2,1)} %all_to_all.20) | data formatting | bytes 12582912
  449.8 38.3 %reduce = bf16[128,24576]{1,0:T(8,128)(2,1)} reduce(bf16[128,1,24576]{2,1,0:T(2,128)(2,1)} %reshape.91, bf16[]{:T(256)} %constant.43), dimensions={1}, to_apply=%all_to_all.13.reduce_sub_computation | reduce | bytes 12582914 | tf_op jit(solution)/shard_map/dispatch/all_to_all | solution.py:51
  488.1 11.2 %reshape.86 = bf16[768,4096]{1,0:T(8,128)(2,1)} reshape(bf16[128,24576]{1,0:T(8,128)(2,1)} %reduce) | data formatting | bytes 12582912 | tf_op jit(solution)/shard_map/expert_ffn/reshape | solution.py:53
  499.3 9.1 %fusion.3 = f32[768,768]{1,0:T(8,128)S(1)} fusion(bf16[768,4096]{1,0:T(8,128)(2,1)} %reshape.86, bf16[1,4096,768]{2,1,0:T(8,128)(2,1)} %param.8), kind=kOutput, calls=%fused_computation.8 | convolution fusion | flops 4831838208 | bytes 14942208 | tf_op jit(solution)/shard_map/expert_ffn/dot_general | solution.py:10
  508.5 8.0 %multiply_convert_fusion = bf16[768,768]{1,0:T(8,128)(2,1)S(1)} fusion(f32[768,768]{1,0:T(8,128)S(1)} %fusion.3, bf16[768,4096]{1,0:T(8,128)(2,1)S(1)} %copy-done.1, bf16[1,4096,768]{2,1,0:T(8,128)(2,1)} %param.9), kind=kOutput, calls=%fused_computation.15 | convolution fusion | flops 4835377152 | bytes 16121856 | tf_op jit(solution)/shard_map/expert_ffn/dot_general | solution.py:11
  516.5 7.1 convolution_convert_fusion.1
  523.6 23.8 %all_to_all.17 = bf16[128,1,24576]{2,1,0:T(2,128)(2,1)} reshape(bf16[768,4096]{1,0:T(8,128)(2,1)} %convolution_convert_fusion.1) | data formatting | bytes 12582912 | tf_op jit(solution)/shard_map/return/all_to_all | solution.py:55
  547.3 38.8 %reduce.3 = bf16[128,24576]{1,0:T(8,128)(2,1)} reduce(bf16[128,1,24576]{2,1,0:T(2,128)(2,1)} %all_to_all.17, bf16[]{:T(256)} %broadcast.85), dimensions={1}, to_apply=%all_to_all.17.reduce_sub_computation | reduce | bytes 12582914 | tf_op jit(solution)/shard_map/return/all_to_all | solution.py:55
  586.2 9.4 %reshape.92 = bf16[128,2,12288]{2,1,0:T(2,128)(2,1)} reshape(bf16[128,24576]{1,0:T(8,128)(2,1)} %reduce.3) | data formatting | bytes 12582912
  595.6 6.9 all-to-all-start.1
  602.6 0.8 select_reduce_fusion
  603.4 74.8 %all-to-all-done.1 = bf16[128,2,12288]{2,1,0:T(2,128)(2,1)} async-done(((bf16[128,2,12288]{2,1,0:T(2,128)(2,1)}), bf16[128,2,12288]{2,1,0:T(2,128)(2,1)}, u32[]{:S(2)}, u32[]{:S(2)}) %all-to-all-start.1) | async-done | bytes 6291488 | tf_op jit(solution)/shard_map/return/all_to_all | solution.py:55
  678.2 33.8 %reshape.93 = bf16[128,1,24576]{2,1,0:T(2,128)(2,1)} reshape(bf16[128,2,12288]{2,1,0:T(2,128)(2,1)} %all-to-all-done.1) | data formatting | bytes 12582912
  712.0 38.3 %reduce.1 = bf16[128,24576]{1,0:T(8,128)(2,1)} reduce(bf16[128,1,24576]{2,1,0:T(2,128)(2,1)} %reshape.93, bf16[]{:T(256)} %constant.43), dimensions={1}, to_apply=%all_to_all.15.reduce_sub_computation | reduce | bytes 12582914 | tf_op jit(solution)/shard_map/return/all_to_all | solution.py:55
  750.3 11.1 %reshape.87 = bf16[768,4096]{1,0:T(8,128)(2,1)} reshape(bf16[128,24576]{1,0:T(8,128)(2,1)} %reduce.1) | data formatting | bytes 12582912 | tf_op jit(solution)/shard_map/return/reshape | solution.py:58
  761.4 3.9 convolution_bitcast_fusion.1
  765.3 7.2 fusion.7
  772.5 6.8 fusion.5
  (30 shorter events, 0.9 us)
Async XLA Ops:
  6.5 248.3 %copy-start = (bf16[96,4096]{1,0:T(8,128)(2,1)S(1)}, bf16[96,4096]{1,0:T(8,128)(2,1)}, u32[]{:S(2)}) copy-start(bf16[96,4096]{1,0:T(8,128)(2,1)} %param.7) | copy-start | bytes 2359300
  6.5 246.7 %all-reduce.5.cloned.1.call-start = ((), (), s32[]{:S(2)}) async-start(), calls=%async_computation.2 | async-start | bytes 37748736 | tf_op jit(solution)/shard_map/hot_weight_broadcast/psum | solution.py:28
  23.1 0.7 copy-start.2
  23.2 738.2 %all-reduce.7.cloned.1.call-start = ((), (), s32[]{:S(2)}) async-start(), calls=%async_computation.3 | async-start | bytes 37748736 | tf_op jit(solution)/shard_map/hot_weight_broadcast/psum | solution.py:27
  488.1 28.4 %slice-start = ((s8[6291456]{0:T(1024)(128)(4,1)}), s8[2097152]{0:T(1024)(128)(4,1)S(1)}, s32[]{:S(2)}) async-start(s8[6291456]{0:T(1024)(128)(4,1)} %bitcast.49), calls=%async_computation.4 | async-start | bytes 4194304
  499.3 9.1 %copy-start.1 = (bf16[768,4096]{1,0:T(8,128)(2,1)S(1)}, bf16[768,4096]{1,0:T(8,128)(2,1)}, u32[]{:S(2)}) copy-start(bf16[768,4096]{1,0:T(8,128)(2,1)} %reshape.86) | copy-start | bytes 18874372
  499.3 17.1 %slice-start.1 = ((s8[6291456]{0:T(1024)(128)(4,1)}), s8[4194304]{0:T(1024)(128)(4,1)S(1)}, s32[]{:S(2)}) async-start(s8[6291456]{0:T(1024)(128)(4,1)} %bitcast.49), calls=%async_computation.5 | async-start | bytes 8388608
  595.6 6.9 copy-start.3
  595.6 82.6 %all-to-all-start.1 = ((bf16[128,2,12288]{2,1,0:T(2,128)(2,1)}), bf16[128,2,12288]{2,1,0:T(2,128)(2,1)}, u32[]{:S(2)}, u32[]{:S(2)}) async-start(bf16[128,2,12288]{2,1,0:T(2,128)(2,1)} %reshape.92), calls=%async_computation.1 | async-start | bytes 12582912 | tf_op jit(solution)/shard_map/return/all_to_all | solution.py:55
Sparse Core Ops, SparseCore 0:
  23.3 229.8 all-reduce.4
  256.3 67.5 all-reduce.6
